TPU v7x, 128 devices: a whole 4x4x4 slice. The times are simulated.
128 devices in a mesh: phase: 8 (over y_hi, z), row: 16 (over x, y_lo, core).
Axes of the slice: x: 4, y: 4 (y_hi: 2, y_lo: 2; y = y_hi * 2 + y_lo), z: 4, core: 2. Of those that a mesh axis runs over, the one named last changes fastest.
Arguments:
- frames: float32 [2, 64, 256, 256], P(None, 'phase', 'row'), may hold values from -50 to 50
- auxiliary: float32 [2, 64, 256, 256], P(None, 'phase', 'row'), may hold values from -6 to 6
- scaled_dual: float32 [2, 64, 256, 256], P(None, 'phase', 'row'), may hold values from -3 to 3
- coil_maps: float32 [16, 2, 256, 256], P(None, None, 'row'), may hold values from -5 to 5
- measured: float32 [16, 2, 64, 256, 256], P(None, None, 'phase', 'row'), may hold values from -6 to 6
- sampling: int32 [64, 256], P('phase'), may hold values 0 or 1
Outputs:
- new_frames: float32 [2, 64, 256, 256], P(None, 'phase', 'row')
- new_aux: float32 [2, 64, 256, 256], P(None, 'phase', 'row')
- new_dual: float32 [2, 64, 256, 256], P(None, 'phase', 'row')
- residual_norms: float32 [2], replicated
All inputs are finite; a program needn't handle non-finite values. No bound on the sum of `sampling` on one device may be relied on, other than what follows from the above.
Results may differ from a plain program's by a relative error of at most 0.003.
Values sent between devices are 32-bit elements; how exact they have to be, the bound alone decides.
No kernel may reach another device: no remote copies, remote signals or barrier semaphores. Data moves between devices by JAX's collectives and lax.ppermute only.
A program may use at most 256 MiB of HBM per device.

v0:
```python
import math
import jax
import jax.numpy as jnp
from jax import lax
from jax.sharding import PartitionSpec as P

CG_STEPS = 2
EXACT = lax.Precision.HIGHEST
PENALTY = 0.5
DAMPING = 0.1
THRESHOLD = 1.0


def padded_2(value, sides, width):
    for axis, dim in sides:
        count, length = (lax.axis_size(axis), value.shape[dim])
        up = [(i, (i + 1) % count) for i in range(count)]
        down = [(j, i) for i, j in up]
        last = lax.slice_in_dim(value, length - width, length, axis=dim)
        initial = lax.slice_in_dim(value, 0, width, axis=dim)
        before = lax.ppermute(last, axis, up)
        after = lax.ppermute(initial, axis, down)
        value = jnp.concatenate([before, value, after], axis=dim)
    return value


def from_behind(value, axis, steps):
    count = lax.axis_size(axis)
    pairs = [(source, (source + steps) % count) for source in range(count)]
    return lax.ppermute(value, axis, pairs)


def tables(count):
    indices = jnp.arange(count, dtype=jnp.int32)
    angles = (indices[:, None] * indices[None, :] % count).astype(jnp.float32) * (
        2.0 * math.pi / count
    )
    return (jnp.cos(angles) / math.sqrt(count), jnp.sin(angles) / math.sqrt(count))


def coil_images(maps, values):
    maps_real = maps[:, 0, None]
    maps_imag = maps[:, 1, None]
    return (
        maps_real * values[0] - maps_imag * values[1],
        maps_real * values[1] + maps_imag * values[0],
    )


def coil_combine(maps, real_part, imag_part):
    maps_real = maps[:, 0, None]
    maps_imag = maps[:, 1, None]
    total_real = jnp.sum(maps_real * real_part + maps_imag * imag_part, 0)
    total_imag = jnp.sum(maps_real * imag_part - maps_imag * real_part, 0)
    return jnp.stack([total_real, total_imag], 0)


def second_diff(values):
    padded = padded_2(values, (("phase", 1),), 1)
    return 2.0 * values - padded[:, 2:] - padded[:, :-2]


def residual_energy(residual):
    return lax.psum(jnp.sum(residual * residual), ("phase", "row"))


def conjugate(estimate, rhs, gram_fn):

    def apply_normal(values):
        return gram_fn(values) + PENALTY * second_diff(values) + DAMPING * values

    residual = rhs - apply_normal(estimate)
    direction = residual
    energy = residual_energy(residual)
    for iteration in range(CG_STEPS):
        image_dir = apply_normal(direction)
        curvature = lax.psum(jnp.sum(direction * image_dir), ("phase", "row"))
        step_size = energy / curvature
        estimate = estimate + step_size * direction
        residual = residual - step_size * image_dir
        if iteration + 1 < CG_STEPS:
            fresh = residual_energy(residual)
            direction = residual + fresh / energy * direction
            energy = fresh
    return estimate


def local(frames, auxiliary, scaled_dual, coil_maps, measured, sampling):
    groups = lax.axis_size("row")
    coil_count = coil_maps.shape[0]
    phases = frames.shape[1]
    row_count = frames.shape[2]
    col_count = frames.shape[3]
    row_total = row_count * groups
    narrow = col_count // groups
    cosine, sine_table = tables(row_total)
    weight = sampling.astype(jnp.float32)[:, None, :]

    def apply_table(values, table):
        return jnp.dot(values, table, precision=EXACT)

    def forward(real_part, imag_part):
        return (
            apply_table(real_part, cosine) + apply_table(imag_part, sine_table),
            apply_table(imag_part, cosine) - apply_table(real_part, sine_table),
        )

    def inverse(real_part, imag_part):
        return (
            apply_table(real_part, cosine) - apply_table(imag_part, sine_table),
            apply_table(imag_part, cosine) + apply_table(real_part, sine_table),
        )

    def filtered(real_part, imag_part):
        spec_real, spec_imag = forward(real_part, imag_part)
        return inverse(spec_real * weight, spec_imag * weight)

    def to_columns_layout(values):
        reshaped = values.reshape(values.shape[:-2] + (row_count, groups, narrow))
        return jnp.moveaxis(reshaped, -3, -1)

    difference = auxiliary - scaled_dual
    previous = from_behind(difference[:, -1:], "phase", 1)
    earlier = jnp.concatenate([previous, difference[:, :-1]], 1)
    rhs_penalty = PENALTY * (earlier - difference)
    moved = (
        lax.all_to_all(
            to_columns_layout(frames.reshape(2 * phases, row_count, col_count)),
            "row",
            split_axis=1,
            concat_axis=3,
            tiled=True,
        ),
        lax.all_to_all(
            to_columns_layout(rhs_penalty.reshape(2 * phases, row_count, col_count)),
            "row",
            split_axis=1,
            concat_axis=3,
            tiled=True,
        ),
        lax.all_to_all(
            to_columns_layout(coil_maps.reshape(2 * coil_count, row_count, col_count)),
            "row",
            split_axis=1,
            concat_axis=3,
            tiled=True,
        ),
        lax.all_to_all(
            to_columns_layout(measured.reshape(coil_count * 2 * phases, row_count, col_count)),
            "row",
            split_axis=1,
            concat_axis=3,
            tiled=True,
        ),
    )
    frames_cols = moved[0].reshape(2, phases, narrow, row_total)
    penalty_cols = moved[1].reshape(2, phases, narrow, row_total)
    maps_cols = moved[2].reshape(coil_count, 2, narrow, row_total)
    measured_cols = moved[3].reshape(coil_count, 2, phases, narrow, row_total)

    def gram_columns(values):
        real_part, imag_part = coil_images(maps_cols, values)
        back_real, back_imag = filtered(real_part, imag_part)
        return coil_combine(maps_cols, back_real, back_imag)

    back_real, back_imag = inverse(measured_cols[:, 0] * weight, measured_cols[:, 1] * weight)
    rhs = coil_combine(maps_cols, back_real, back_imag) + penalty_cols
    solved = conjugate(frames_cols, rhs, gram_columns)
    values = solved.reshape(2 * phases, narrow, row_total)
    reshaped = values.reshape(values.shape[:-2] + (narrow, groups, row_count))
    returned = lax.all_to_all(
        jnp.moveaxis(reshaped, -3, -1), "row", split_axis=1, concat_axis=3, tiled=True
    )
    estimate = returned.reshape(2, phases, row_count, col_count)
    following = from_behind(estimate[:, :1], "phase", -1)
    advanced = jnp.concatenate([estimate[:, 1:], following], 1)
    shifted = advanced - estimate + scaled_dual
    magnitude = jnp.sqrt(shifted[0] * shifted[0] + shifted[1] * shifted[1])
    factor = jnp.maximum(magnitude - THRESHOLD, 0.0) / jnp.maximum(magnitude, THRESHOLD)
    new_aux = shifted * factor[None]
    new_dual = shifted - new_aux
    primal_gap = new_dual - scaled_dual
    dual_gap = new_aux - auxiliary
    primal_sum, dual_sum = lax.psum(
        (jnp.sum(primal_gap * primal_gap), jnp.sum(dual_gap * dual_gap)), ("phase", "row")
    )
    residual_norms = jnp.stack([jnp.sqrt(primal_sum), PENALTY * jnp.sqrt(dual_sum)])
    return (estimate, new_aux, new_dual, residual_norms)


def solution(mesh):
    in_specs = (
        P(None, "phase", "row", None),
        P(None, "phase", "row", None),
        P(None, "phase", "row", None),
        P(None, None, "row", None),
        P(None, None, "phase", "row", None),
        P("phase", None),
    )
    out_specs = (
        P(None, "phase", "row", None),
        P(None, "phase", "row", None),
        P(None, "phase", "row", None),
        P(),
    )
    return jax.shard_map(local, mesh=mesh, in_specs=in_specs, out_specs=out_specs, check_vma=False)
```

profile of v0, /device:TPU:1, one launch (start us, length us, event | category | flops | bytes accessed | tf_op | source)
XLA Modules:
  0.0 575.1 jit_solution(8731979419725957966)
XLA Ops:
  4.2 2.9 reshape_reshape.15
  10.5 6.3 %all-to-all-start = ((f32[16,1,4096]{2,1,0:T(1,128)}), f32[16,1,4096]{2,1,0:T(1,128)S(1)}, u32[]{:S(2)}, u32[]{:S(2)}) async-start(f32[16,1,4096]{2,1,0:T(1,128)} %reshape.40), calls=%async_computation | async-start | bytes 524288 | tf_op jit(solution)/shard_map/all_to_all | solution.py:127
  19.5 3.0 reshape.42
  24.2 4.1 all-to-all-start.3
  30.9 4.0 copy.28
  36.7 6.3 %all-to-all-start.1 = ((f32[16,1,8192]{2,1,0:T(1,128)}), f32[16,1,8192]{2,1,0:T(1,128)S(1)}, u32[]{:S(2)}, u32[]{:S(2)}) async-start(f32[16,1,8192]{2,1,0:T(1,128)} %reshape.44), calls=%async_computation.1 | async-start | bytes 1048576 | tf_op jit(solution)/shard_map/all_to_all | solution.py:141
  43.1 19.4 %reshape_reshape.17 = f32[256,16,16,16]{3,2,1,0:T(8,128)} reshape(f32[16,2,8,16,256]{4,3,2,1,0:T(8,128)} %param.10) | data formatting | bytes 8388608 | tf_op jit(solution)/shard_map/reshape;reshape | solution.py:119
  62.5 21.3 %copy.30 = f32[256,16,16,16]{0,3,2,1:T(8,128)} copy(f32[256,16,16,16]{2,1,3,0:T(8,128)} %bitcast.200) | data formatting | bytes 8388608 | tf_op jit(solution)/shard_map/transpose | solution.py:120
  88.5 5.7 all-to-all-start.2
  102.9 4.2 collective-permute-start.1
  120.9 4.4 copy.29
  125.3 3.7 reshape.34
  129.0 2.9 fusion.10
  131.9 2.9 fusion.11
  134.8 3.0 subtract_multiply_fusion.2
  137.8 4.1 fusion.129
  141.9 3.3 add_multiply_fusion.2
  145.3 2.8 fusion.132
  148.1 4.1 convolution_subtract_fusion.2
  152.2 26.4 %copy.31 = f32[256,1,16,16,16]{4,3,2,0,1:T(8,128)} copy(f32[256,1,16,16,16]{0,4,2,3,1:T(8,128)} %bitcast.9) | data formatting | bytes 8388608 | tf_op jit(solution)/shard_map/all_to_all | solution.py:148
  178.6 23.6 %reshape.35 = f32[16,2,8,16,256]{4,3,2,1,0:T(8,128)} reshape(f32[256,1,16,16,16]{4,3,2,0,1:T(8,128)} %copy.31) | data formatting | bytes 8388608 | tf_op jit(solution)/shard_map/reshape | solution.py:159
  202.3 4.6 fusion.14
  206.9 2.9 fusion.16
  209.8 2.9 fusion.25
  212.7 3.0 fusion.22
  215.7 4.3 add_reduce_fusion.2
  220.9 2.9 fusion.7
  223.9 2.9 fusion.6
  226.7 5.1 collective-permute-start.3
  232.3 3.0 add_multiply_fusion.1
  235.3 2.9 fusion.126
  238.2 3.0 subtract_multiply_fusion.1
  241.1 2.9 fusion.123
  244.0 3.1 convolution_subtract_fusion.1
  247.1 3.4 add_reduce_fusion.1
  251.3 67.4 %all-reduce.1 = (f32[]{:T(128)}, f32[]{:T(128)}) all-reduce(f32[]{:T(128)} %get-tuple-element.15, f32[]{:T(128)} %get-tuple-element.14), channel_id=1, replica_groups=mesh['phase'=8,'row'=16] {'phase','row'}, use_global_device_ids=true, to_apply=%region_5.6 | all-reduce | flops 2 | bytes 16 | tf_op jit(solution)/shard_map/psum | solution.py:64
  320.7 62.7 %psum.44 = f32[]{:T(128)} all-reduce(f32[]{:T(128)} %multiply_reduce_fusion.2), channel_id=1, replica_groups=mesh['phase'=8,'row'=16] {'phase','row'}, use_global_device_ids=true, to_apply=%region_11.12 | all-reduce | flops 1 | bytes 8 | tf_op jit(solution)/shard_map/psum | solution.py:64
  384.9 2.9 fusion.3
  387.9 2.9 fusion.2
  394.0 3.0 add_multiply_fusion
  397.0 2.8 fusion.120
  399.8 3.1 subtract_multiply_fusion
  402.9 2.8 fusion.117
  405.7 3.1 convolution_subtract_fusion
  408.8 3.4 add_reduce_fusion
  412.9 66.4 %psum.45 = f32[]{:T(128)} all-reduce(f32[]{:T(128)} %fusion.88), channel_id=1, replica_groups=mesh['phase'=8,'row'=16] {'phase','row'}, use_global_device_ids=true, to_apply=%region_15.16 | all-reduce | flops 1 | bytes 8 | tf_op jit(solution)/shard_map/psum | solution.py:77
  485.8 11.3 %all_to_all.75 = f32[16,1,4096]{2,1,0:T(1,128)S(1)} all-to-all(f32[16,1,4096]{2,1,0:T(1,128)S(1)} %reshape.46), channel_id=1, replica_groups=mesh['phase'=8,'row'=16] {'row'}, dimensions={0} | all-to-all | bytes 524288 | tf_op jit(solution)/shard_map/all_to_all | solution.py:171
  506.9 66.1 %all-reduce = (f32[]{:T(128)}, f32[]{:T(128)}) all-reduce(f32[]{:T(128)} %multiply_reduce_fusion, f32[]{:T(128)} %get-tuple-element.20), channel_id=1, replica_groups=mesh['phase'=8,'row'=16] {'phase','row'}, use_global_device_ids=true, to_apply=%region_19.20 | all-reduce | flops 2 | bytes 16 | tf_op jit(solution)/shard_map/psum | solution.py:184
  (101 shorter events, 64.9 us)
Async XLA Ops:
  1.7 15.1 %collective-permute-start = (f32[2,1,16,256]{3,2,1,0:T(8,128)S(1)}, f32[2,1,16,256]{3,2,1,0:T(8,128)S(1)}, u32[]{:S(2)}, u32[]{:S(2)}) collective-permute-start(f32[2,1,16,256]{3,2,1,0:T(8,128)S(1)} %slice.144), channel_id=1, source_target_pairs={{0,16},{16,32},{32,48},{48,64},{64,80},{80,96},{96,112},{112,0},{1... | collective-permute-start | bytes 98312 | tf_op jit(solution)/shard_map/ppermute | solution.py:30
  10.5 13.7 %all-to-all-start = ((f32[16,1,4096]{2,1,0:T(1,128)}), f32[16,1,4096]{2,1,0:T(1,128)S(1)}, u32[]{:S(2)}, u32[]{:S(2)}) async-start(f32[16,1,4096]{2,1,0:T(1,128)} %reshape.40), calls=%async_computation | async-start | bytes 524288 | tf_op jit(solution)/shard_map/all_to_all | solution.py:127
  19.5 8.8 %copy-start.11 = (f32[16,2,16,256]{3,2,1,0:T(8,128)S(1)}, f32[16,2,16,256]{3,2,1,0:T(8,128)}, u32[]{:S(2)}) copy-start(f32[16,2,16,256]{3,2,1,0:T(8,128)} %param.9) | copy-start | bytes 1572868
  24.2 12.5 %all-to-all-start.3 = ((f32[16,1,4096]{2,1,0:T(1,128)}), f32[16,1,4096]{2,1,0:T(1,128)S(1)}, u32[]{:S(2)}, u32[]{:S(2)}) async-start(f32[16,1,4096]{2,1,0:T(1,128)} %reshape.42), calls=%async_computation.3 | async-start | bytes 524288 | tf_op jit(solution)/shard_map/all_to_all | solution.py:134
  35.0 8.1 %copy-start.12 = (s32[8,256]{1,0:T(8,128)S(1)}, s32[8,256]{1,0:T(8,128)}, u32[]{:S(2)}) copy-start(s32[8,256]{1,0:T(8,128)} %param.11) | copy-start | bytes 24580
  36.7 25.8 %copy-start.8 = (f32[16,1,4096]{2,1,0:T(1,128)}, f32[16,1,4096]{2,1,0:T(1,128)S(1)}, u32[]{:S(2)}) copy-start(f32[16,1,4096]{2,1,0:T(1,128)S(1)} %all-to-all-done.3) | copy-start | bytes 786436
  36.7 51.0 %all-to-all-start.1 = ((f32[16,1,8192]{2,1,0:T(1,128)}), f32[16,1,8192]{2,1,0:T(1,128)S(1)}, u32[]{:S(2)}, u32[]{:S(2)}) async-start(f32[16,1,8192]{2,1,0:T(1,128)} %reshape.44), calls=%async_computation.1 | async-start | bytes 1048576 | tf_op jit(solution)/shard_map/all_to_all | solution.py:141
  87.7 0.8 copy-start.5
  88.5 63.7 %all-to-all-start.2 = ((f32[256,16,16,16]{0,3,2,1:T(8,128)}), f32[256,16,16,16]{0,3,2,1:T(8,128)}, u32[]{:S(2)}, u32[]{:S(2)}) async-start(f32[256,16,16,16]{0,3,2,1:T(8,128)} %copy.30), calls=%async_computation.2 | async-start | bytes 8388608 | tf_op jit(solution)/shard_map/all_to_all | solution.py:148
  101.8 6.5 %copy-start.9 = (f32[16,1,4096]{2,1,0:T(1,128)S(1)}, f32[16,1,4096]{2,1,0:T(1,128)}, u32[]{:S(2)}) copy-start(f32[16,1,4096]{2,1,0:T(1,128)} %copy-done.8) | copy-start | bytes 786436
  102.9 117.1 %collective-permute-start.1 = (f32[2,1,16,256]{3,2,1,0:T(8,128)}, f32[2,1,16,256]{3,2,1,0:T(8,128)}, u32[]{:S(2)}, u32[]{:S(2)}) collective-permute-start(f32[2,1,16,256]{3,2,1,0:T(8,128)} %get-tuple-element.35), channel_id=1, source_target_pairs={{16,0},{32,16},{48,32},{64,48},{80,64},{96,80},{112,96},{0,112},{1... | collective-permute-start | bytes 98312 | tf_op jit(solution)/shard_map/ppermute | solution.py:22
  107.1 112.9 %collective-permute-start.2 = (f32[2,1,16,256]{3,2,1,0:T(8,128)}, f32[2,1,16,256]{3,2,1,0:T(8,128)}, u32[]{:S(2)}, u32[]{:S(2)}) collective-permute-start(f32[2,1,16,256]{3,2,1,0:T(8,128)} %get-tuple-element.36), channel_id=1, source_target_pairs={{0,16},{16,32},{32,48},{48,64},{64,80},{80,96},{96,112},{112,0},{1... | collective-permute-start | bytes 98312 | tf_op jit(solution)/shard_map/ppermute | solution.py:21
  114.1 1.0 copy-start.6
  202.3 4.6 copy-start
  212.7 3.0 copy-start.1
  212.7 3.0 copy-start.2
  226.7 23.8 %collective-permute-start.3 = (f32[2,1,16,256]{3,2,1,0:T(8,128)S(1)}, f32[2,1,16,256]{3,2,1,0:T(8,128)S(1)}, u32[]{:S(2)}, u32[]{:S(2)}) collective-permute-start(f32[2,1,16,256]{3,2,1,0:T(8,128)S(1)} %get-tuple-element.33), channel_id=1, source_target_pairs={{16,0},{32,16},{48,32},{64,48},{80,64},{96,80},{112,96},{0,112},{1... | collective-permute-start | bytes 98312 | tf_op jit(solution)/shard_map/ppermute | solution.py:22
  231.9 18.6 %collective-permute-start.4 = (f32[2,1,16,256]{3,2,1,0:T(8,128)S(1)}, f32[2,1,16,256]{3,2,1,0:T(8,128)S(1)}, u32[]{:S(2)}, u32[]{:S(2)}) collective-permute-start(f32[2,1,16,256]{3,2,1,0:T(8,128)S(1)} %get-tuple-element.34), channel_id=1, source_target_pairs={{0,16},{16,32},{32,48},{48,64},{64,80},{80,96},{96,112},{112,0},{1... | collective-permute-start | bytes 98312 | tf_op jit(solution)/shard_map/ppermute | solution.py:21
  390.8 21.4 %collective-permute-start.5 = (f32[2,1,16,256]{3,2,1,0:T(8,128)S(1)}, f32[2,1,16,256]{3,2,1,0:T(8,128)S(1)}, u32[]{:S(2)}, u32[]{:S(2)}) collective-permute-start(f32[2,1,16,256]{3,2,1,0:T(8,128)S(1)} %get-tuple-element.29), channel_id=1, source_target_pairs={{16,0},{32,16},{48,32},{64,48},{80,64},{96,80},{112,96},{0,112},{1... | collective-permute-start | bytes 98312 | tf_op jit(solution)/shard_map/ppermute | solution.py:22
  393.6 18.7 %collective-permute-start.6 = (f32[2,1,16,256]{3,2,1,0:T(8,128)S(1)}, f32[2,1,16,256]{3,2,1,0:T(8,128)S(1)}, u32[]{:S(2)}, u32[]{:S(2)}) collective-permute-start(f32[2,1,16,256]{3,2,1,0:T(8,128)S(1)} %get-tuple-element.30), channel_id=1, source_target_pairs={{0,16},{16,32},{32,48},{48,64},{64,80},{80,96},{96,112},{112,0},{1... | collective-permute-start | bytes 98312 | tf_op jit(solution)/shard_map/ppermute | solution.py:21
  500.4 4.3 copy-start.4
  501.4 73.5 %copy-start.3 = (f32[2,8,16,256]{3,2,1,0:T(8,128)}, f32[2,8,16,256]{3,2,1,0:T(8,128)S(1)}, u32[]{:S(2)}) copy-start(f32[2,8,16,256]{3,2,1,0:T(8,128)S(1)} %reshape.37) | copy-start | bytes 786436
  501.4 4.8 copy-start.7
  501.4 3.3 collective-permute-start.7
  506.2 68.7 %copy-start.10 = (f32[2,8,16,256]{3,2,1,0:T(8,128)}, f32[2,8,16,256]{3,2,1,0:T(8,128)S(1)}, u32[]{:S(2)}) copy-start(f32[2,8,16,256]{3,2,1,0:T(8,128)S(1)} %get-tuple-element.22) | copy-start | bytes 786436
where the time goes:
time: 583 us; the launch traced here: 575 us
  blocking collectives  274 us (47%)
  local copies, waits for them, and re-layouts  150 us (26%)
  matrix products  88.7 us (15%)
  starting transfers between devices  40.4 us (7%)
  other arithmetic  12.8 us (2%)
  between operations  6.86 us (1%)
    psum x2, blocking collectives, residual_energy(): return lax.psum(jnp.sum(residual * residual), ('phase', 'row'))  130 us
    dot_general x28, matrix products, apply_table(): return jnp.dot(values, table, precision=EXACT)  88.7 us
    psum x1, blocking collectives, conjugate(): curvature = lax.psum(jnp.sum(direction * image_dir), ('phase', 'row'))  66.4 us
    psum x1, blocking collectives, local(): lax.psum((jnp.sum(primal_gap * primal_gap), jnp.sum(dual_gap * dual_gap))...  66.1 us
    transpose x4, local copies, waits for them, and re-layouts, to_columns_layout(): return jnp.moveaxis(reshaped, -3, -1)  29.3 us
    all_to_all x1, local copies, waits for them, and re-layouts, local(): lax.all_to_all(to_columns_layout(measured.reshape(coil_count * 2 * phases...  26.4 us
    another operation x4, local copies, waits for them, and re-layouts, to_columns_layout(): reshaped = values.reshape(values.shape[:-2] + (row_count, groups, narrow))  25.6 us
    reshape x1, local copies, waits for them, and re-layouts, local(): measured_cols = moved[3].reshape(coil_count, 2, phases, narrow, row_total)  23.6 us
  transfers between devices with their start and end apart: 12, of which 2 were waited for; matrix products, arithmetic and copies ran while one was open for 39% of the time, Pallas kernels for 0%

commit v1 on v0

--- a/solution.py
+++ b/solution.py
@@ -182,7 +182,7 @@
     primal_gap = new_dual - scaled_dual
     dual_gap = new_aux - auxiliary
     primal_sum, dual_sum = lax.psum(
-        (jnp.sum(primal_gap * primal_gap), jnp.sum(dual_gap * dual_gap)), ("phase", "row")
+        lax.psum((jnp.sum(primal_gap * primal_gap), jnp.sum(dual_gap * dual_gap)), "phase"), "row"
     )
     residual_norms = jnp.stack([jnp.sqrt(primal_sum), PENALTY * jnp.sqrt(dual_sum)])
     return (estimate, new_aux, new_dual, residual_norms)

time: 583 us -> 571 us (0.979)
  blocking collectives: 274 us -> 262 us
    psum x1, blocking collectives: 66.1 us -> 21.4 us  [local(): lax.psum((jnp.sum(primal_gap * primal_gap), jnp.sum(dual_gap * dual_gap))...]
    psum x0 -> x1, blocking collectives: none -> 32.5 us  [local(): lax.psum(lax.psum((jnp.sum(primal_gap * primal_gap), jnp.sum(dual_gap * d...]
where the time goes in v1:
time: 571 us; the launch traced here: 563 us
  blocking collectives  262 us (46%)
  local copies, waits for them, and re-layouts  150 us (26%)
  matrix products  88.7 us (16%)
  starting transfers between devices  40.4 us (7%)
  other arithmetic  12.8 us (2%)
  between operations  6.99 us (1%)
    psum x2, blocking collectives, residual_energy(): return lax.psum(jnp.sum(residual * residual), ('phase', 'row'))  130 us
    dot_general x28, matrix products, apply_table(): return jnp.dot(values, table, precision=EXACT)  88.7 us
    psum x1, blocking collectives, conjugate(): curvature = lax.psum(jnp.sum(direction * image_dir), ('phase', 'row'))  66.4 us
    psum x1, blocking collectives, local(): lax.psum(lax.psum((jnp.sum(primal_gap * primal_gap), jnp.sum(dual_gap * d...  32.5 us
    transpose x4, local copies, waits for them, and re-layouts, to_columns_layout(): return jnp.moveaxis(reshaped, -3, -1)  29.3 us
    all_to_all x1, local copies, waits for them, and re-layouts, local(): lax.all_to_all(to_columns_layout(measured.reshape(coil_count * 2 * phases...  26.4 us
    another operation x4, local copies, waits for them, and re-layouts, to_columns_layout(): reshaped = values.reshape(values.shape[:-2] + (row_count, groups, narrow))  25.6 us
    reshape x1, local copies, waits for them, and re-layouts, local(): measured_cols = moved[3].reshape(coil_count, 2, phases, narrow, row_total)  23.6 us
  transfers between devices with their start and end apart: 12, of which 2 were waited for; matrix products, arithmetic and copies ran while one was open for 39% of the time, Pallas kernels for 0%

profile of v1, /device:TPU:1, one launch (start us, length us, event | category | flops | bytes accessed | tf_op | source)
XLA Modules:
  0.0 563.1 jit_solution(15008643688367578190)
XLA Ops:
  4.2 2.9 reshape_reshape.15
  10.5 6.3 %all-to-all-start = ((f32[16,1,4096]{2,1,0:T(1,128)}), f32[16,1,4096]{2,1,0:T(1,128)S(1)}, u32[]{:S(2)}, u32[]{:S(2)}) async-start(f32[16,1,4096]{2,1,0:T(1,128)} %reshape.40), calls=%async_computation | async-start | bytes 524288 | tf_op jit(solution)/shard_map/all_to_all | solution.py:127
  19.5 3.0 reshape.42
  24.2 4.1 all-to-all-start.3
  30.9 4.0 copy.28
  36.7 6.3 %all-to-all-start.1 = ((f32[16,1,8192]{2,1,0:T(1,128)}), f32[16,1,8192]{2,1,0:T(1,128)S(1)}, u32[]{:S(2)}, u32[]{:S(2)}) async-start(f32[16,1,8192]{2,1,0:T(1,128)} %reshape.44), calls=%async_computation.1 | async-start | bytes 1048576 | tf_op jit(solution)/shard_map/all_to_all | solution.py:141
  43.1 19.4 %reshape_reshape.17 = f32[256,16,16,16]{3,2,1,0:T(8,128)} reshape(f32[16,2,8,16,256]{4,3,2,1,0:T(8,128)} %param.10) | data formatting | bytes 8388608 | tf_op jit(solution)/shard_map/reshape;reshape | solution.py:119
  62.5 21.3 %copy.30 = f32[256,16,16,16]{0,3,2,1:T(8,128)} copy(f32[256,16,16,16]{2,1,3,0:T(8,128)} %bitcast.200) | data formatting | bytes 8388608 | tf_op jit(solution)/shard_map/transpose | solution.py:120
  88.5 5.7 %all-to-all-start.2 = ((f32[256,16,16,16]{0,3,2,1:T(8,128)}), f32[256,16,16,16]{0,3,2,1:T(8,128)}, u32[]{:S(2)}, u32[]{:S(2)}) async-start(f32[256,16,16,16]{0,3,2,1:T(8,128)} %copy.30), calls=%async_computation.2 | async-start | bytes 8388608 | tf_op jit(solution)/shard_map/all_to_all | solution.py:148
  102.9 4.2 collective-permute-start.1
  120.9 4.4 copy.29
  125.3 3.7 reshape.34
  129.0 2.9 fusion.10
  131.9 2.9 fusion.11
  134.8 3.0 subtract_multiply_fusion.2
  137.8 4.1 fusion.129
  141.9 3.3 add_multiply_fusion.2
  148.1 4.1 convolution_subtract_fusion.2
  152.2 26.4 %copy.31 = f32[256,1,16,16,16]{4,3,2,0,1:T(8,128)} copy(f32[256,1,16,16,16]{0,4,2,3,1:T(8,128)} %bitcast.9) | data formatting | bytes 8388608 | tf_op jit(solution)/shard_map/all_to_all | solution.py:148
  178.6 23.6 %reshape.35 = f32[16,2,8,16,256]{4,3,2,1,0:T(8,128)} reshape(f32[256,1,16,16,16]{4,3,2,0,1:T(8,128)} %copy.31) | data formatting | bytes 8388608 | tf_op jit(solution)/shard_map/reshape | solution.py:159
  202.3 4.6 fusion.14
  206.9 2.9 fusion.16
  209.8 2.9 fusion.25
  212.7 3.0 fusion.22
  215.7 4.3 add_reduce_fusion.2
  220.9 2.9 fusion.7
  223.9 2.9 fusion.6
  226.7 5.1 collective-permute-start.3
  232.3 3.0 add_multiply_fusion.1
  235.3 2.9 fusion.126
  238.2 3.0 subtract_multiply_fusion.1
  241.1 2.9 fusion.123
  244.0 3.1 convolution_subtract_fusion.1
  247.1 3.4 add_reduce_fusion.1
  251.3 67.4 %all-reduce = (f32[]{:T(128)}, f32[]{:T(128)}) all-reduce(f32[]{:T(128)} %get-tuple-element.15, f32[]{:T(128)} %get-tuple-element.14), channel_id=1, replica_groups=mesh['phase'=8,'row'=16] {'phase','row'}, use_global_device_ids=true, to_apply=%region_5.6 | all-reduce | flops 2 | bytes 16 | tf_op jit(solution)/shard_map/psum | solution.py:64
  320.7 62.7 %psum.58 = f32[]{:T(128)} all-reduce(f32[]{:T(128)} %multiply_reduce_fusion.2), channel_id=1, replica_groups=mesh['phase'=8,'row'=16] {'phase','row'}, use_global_device_ids=true, to_apply=%region_11.12 | all-reduce | flops 1 | bytes 8 | tf_op jit(solution)/shard_map/psum | solution.py:64
  384.9 2.9 fusion.3
  387.9 2.9 fusion.2
  394.0 3.0 add_multiply_fusion
  396.9 2.9 fusion.120
  399.8 3.1 subtract_multiply_fusion
  402.9 2.9 fusion.117
  405.7 3.1 convolution_subtract_fusion
  408.8 3.4 add_reduce_fusion
  412.9 66.4 %psum.59 = f32[]{:T(128)} all-reduce(f32[]{:T(128)} %fusion.88), channel_id=1, replica_groups=mesh['phase'=8,'row'=16] {'phase','row'}, use_global_device_ids=true, to_apply=%region_15.16 | all-reduce | flops 1 | bytes 8 | tf_op jit(solution)/shard_map/psum | solution.py:77
  485.8 11.3 %all_to_all.75 = f32[16,1,4096]{2,1,0:T(1,128)S(1)} all-to-all(f32[16,1,4096]{2,1,0:T(1,128)S(1)} %reshape.46), channel_id=1, replica_groups=mesh['phase'=8,'row'=16] {'row'}, dimensions={0} | all-to-all | bytes 524288 | tf_op jit(solution)/shard_map/all_to_all | solution.py:171
  506.9 21.4 %all-reduce.2 = (f32[]{:T(128)}, f32[]{:T(128)}) all-reduce(f32[]{:T(128)} %multiply_reduce_fusion, f32[]{:T(128)} %get-tuple-element.22), channel_id=1, replica_groups=mesh['phase'=8,'row'=16] {'phase'}, use_global_device_ids=true, to_apply=%region_20.21 | all-reduce | flops 2 | bytes 16 | tf_op jit(solution)/shard_map/psum | solution.py:185
  528.3 32.5 %all-reduce.1 = (f32[]{:T(128)}, f32[]{:T(128)}) all-reduce(f32[]{:T(128)} %get-tuple-element.20, f32[]{:T(128)} %get-tuple-element.21), channel_id=1, replica_groups=mesh['phase'=8,'row'=16] {'row'}, use_global_device_ids=true, to_apply=%region_21.22 | all-reduce | flops 2 | bytes 16 | tf_op jit(solution)/shard_map/psum | solution.py:184
  (102 shorter events, 67.8 us)
Async XLA Ops:
  1.7 15.1 %collective-permute-start = (f32[2,1,16,256]{3,2,1,0:T(8,128)S(1)}, f32[2,1,16,256]{3,2,1,0:T(8,128)S(1)}, u32[]{:S(2)}, u32[]{:S(2)}) collective-permute-start(f32[2,1,16,256]{3,2,1,0:T(8,128)S(1)} %slice.144), channel_id=1, source_target_pairs={{0,16},{16,32},{32,48},{48,64},{64,80},{80,96},{96,112},{112,0},{1... | collective-permute-start | bytes 98312 | tf_op jit(solution)/shard_map/ppermute | solution.py:30
  10.5 13.7 %all-to-all-start = ((f32[16,1,4096]{2,1,0:T(1,128)}), f32[16,1,4096]{2,1,0:T(1,128)S(1)}, u32[]{:S(2)}, u32[]{:S(2)}) async-start(f32[16,1,4096]{2,1,0:T(1,128)} %reshape.40), calls=%async_computation | async-start | bytes 524288 | tf_op jit(solution)/shard_map/all_to_all | solution.py:127
  19.5 8.8 %copy-start.11 = (f32[16,2,16,256]{3,2,1,0:T(8,128)S(1)}, f32[16,2,16,256]{3,2,1,0:T(8,128)}, u32[]{:S(2)}) copy-start(f32[16,2,16,256]{3,2,1,0:T(8,128)} %param.9) | copy-start | bytes 1572868
  24.2 12.5 %all-to-all-start.3 = ((f32[16,1,4096]{2,1,0:T(1,128)}), f32[16,1,4096]{2,1,0:T(1,128)S(1)}, u32[]{:S(2)}, u32[]{:S(2)}) async-start(f32[16,1,4096]{2,1,0:T(1,128)} %reshape.42), calls=%async_computation.3 | async-start | bytes 524288 | tf_op jit(solution)/shard_map/all_to_all | solution.py:134
  35.0 8.1 %copy-start.12 = (s32[8,256]{1,0:T(8,128)S(1)}, s32[8,256]{1,0:T(8,128)}, u32[]{:S(2)}) copy-start(s32[8,256]{1,0:T(8,128)} %param.11) | copy-start | bytes 24580
  36.7 25.8 %copy-start.8 = (f32[16,1,4096]{2,1,0:T(1,128)}, f32[16,1,4096]{2,1,0:T(1,128)S(1)}, u32[]{:S(2)}) copy-start(f32[16,1,4096]{2,1,0:T(1,128)S(1)} %all-to-all-done.3) | copy-start | bytes 786436
  36.7 51.0 %all-to-all-start.1 = ((f32[16,1,8192]{2,1,0:T(1,128)}), f32[16,1,8192]{2,1,0:T(1,128)S(1)}, u32[]{:S(2)}, u32[]{:S(2)}) async-start(f32[16,1,8192]{2,1,0:T(1,128)} %reshape.44), calls=%async_computation.1 | async-start | bytes 1048576 | tf_op jit(solution)/shard_map/all_to_all | solution.py:141
  87.7 0.8 copy-start.5
  88.5 63.7 %all-to-all-start.2 = ((f32[256,16,16,16]{0,3,2,1:T(8,128)}), f32[256,16,16,16]{0,3,2,1:T(8,128)}, u32[]{:S(2)}, u32[]{:S(2)}) async-start(f32[256,16,16,16]{0,3,2,1:T(8,128)} %copy.30), calls=%async_computation.2 | async-start | bytes 8388608 | tf_op jit(solution)/shard_map/all_to_all | solution.py:148
  101.8 6.5 %copy-start.9 = (f32[16,1,4096]{2,1,0:T(1,128)S(1)}, f32[16,1,4096]{2,1,0:T(1,128)}, u32[]{:S(2)}) copy-start(f32[16,1,4096]{2,1,0:T(1,128)} %copy-done.8) | copy-start | bytes 786436
  102.9 117.1 %collective-permute-start.1 = (f32[2,1,16,256]{3,2,1,0:T(8,128)}, f32[2,1,16,256]{3,2,1,0:T(8,128)}, u32[]{:S(2)}, u32[]{:S(2)}) collective-permute-start(f32[2,1,16,256]{3,2,1,0:T(8,128)} %get-tuple-element.37), channel_id=1, source_target_pairs={{16,0},{32,16},{48,32},{64,48},{80,64},{96,80},{112,96},{0,112},{1... | collective-permute-start | bytes 98312 | tf_op jit(solution)/shard_map/ppermute | solution.py:22
  107.1 112.9 %collective-permute-start.2 = (f32[2,1,16,256]{3,2,1,0:T(8,128)}, f32[2,1,16,256]{3,2,1,0:T(8,128)}, u32[]{:S(2)}, u32[]{:S(2)}) collective-permute-start(f32[2,1,16,256]{3,2,1,0:T(8,128)} %get-tuple-element.38), channel_id=1, source_target_pairs={{0,16},{16,32},{32,48},{48,64},{64,80},{80,96},{96,112},{112,0},{1... | collective-permute-start | bytes 98312 | tf_op jit(solution)/shard_map/ppermute | solution.py:21
  114.1 1.0 copy-start.6
  202.3 4.6 copy-start
  212.7 3.0 copy-start.1
  212.7 3.0 copy-start.2
  226.7 23.8 %collective-permute-start.3 = (f32[2,1,16,256]{3,2,1,0:T(8,128)S(1)}, f32[2,1,16,256]{3,2,1,0:T(8,128)S(1)}, u32[]{:S(2)}, u32[]{:S(2)}) collective-permute-start(f32[2,1,16,256]{3,2,1,0:T(8,128)S(1)} %get-tuple-element.35), channel_id=1, source_target_pairs={{16,0},{32,16},{48,32},{64,48},{80,64},{96,80},{112,96},{0,112},{1... | collective-permute-start | bytes 98312 | tf_op jit(solution)/shard_map/ppermute | solution.py:22
  231.9 18.6 %collective-permute-start.4 = (f32[2,1,16,256]{3,2,1,0:T(8,128)S(1)}, f32[2,1,16,256]{3,2,1,0:T(8,128)S(1)}, u32[]{:S(2)}, u32[]{:S(2)}) collective-permute-start(f32[2,1,16,256]{3,2,1,0:T(8,128)S(1)} %get-tuple-element.36), channel_id=1, source_target_pairs={{0,16},{16,32},{32,48},{48,64},{64,80},{80,96},{96,112},{112,0},{1... | collective-permute-start | bytes 98312 | tf_op jit(solution)/shard_map/ppermute | solution.py:21
  390.8 21.5 %collective-permute-start.5 = (f32[2,1,16,256]{3,2,1,0:T(8,128)S(1)}, f32[2,1,16,256]{3,2,1,0:T(8,128)S(1)}, u32[]{:S(2)}, u32[]{:S(2)}) collective-permute-start(f32[2,1,16,256]{3,2,1,0:T(8,128)S(1)} %get-tuple-element.31), channel_id=1, source_target_pairs={{16,0},{32,16},{48,32},{64,48},{80,64},{96,80},{112,96},{0,112},{1... | collective-permute-start | bytes 98312 | tf_op jit(solution)/shard_map/ppermute | solution.py:22
  393.6 18.7 %collective-permute-start.6 = (f32[2,1,16,256]{3,2,1,0:T(8,128)S(1)}, f32[2,1,16,256]{3,2,1,0:T(8,128)S(1)}, u32[]{:S(2)}, u32[]{:S(2)}) collective-permute-start(f32[2,1,16,256]{3,2,1,0:T(8,128)S(1)} %get-tuple-element.32), channel_id=1, source_target_pairs={{0,16},{16,32},{32,48},{48,64},{64,80},{80,96},{96,112},{112,0},{1... | collective-permute-start | bytes 98312 | tf_op jit(solution)/shard_map/ppermute | solution.py:21
  500.4 4.3 copy-start.4
  501.3 61.5 %copy-start.3 = (f32[2,8,16,256]{3,2,1,0:T(8,128)}, f32[2,8,16,256]{3,2,1,0:T(8,128)S(1)}, u32[]{:S(2)}) copy-start(f32[2,8,16,256]{3,2,1,0:T(8,128)S(1)} %reshape.37) | copy-start | bytes 786436
  501.3 4.8 copy-start.7
  501.4 3.3 collective-permute-start.7
  506.2 56.6 %copy-start.10 = (f32[2,8,16,256]{3,2,1,0:T(8,128)}, f32[2,8,16,256]{3,2,1,0:T(8,128)S(1)}, u32[]{:S(2)}) copy-start(f32[2,8,16,256]{3,2,1,0:T(8,128)S(1)} %get-tuple-element.24) | copy-start | bytes 786436
